TPU v7x, 512 devices: a whole 4x8x8 slice. The times are simulated.
512 devices in a mesh: req: 64 (over x, y, core), head: 8 (over z).
Axes of the slice: x: 4, y: 8, z: 8, core: 2. Of those that a mesh axis runs over, the one named last changes fastest.
Arguments:
- hidden: bfloat16 [512, 4096], P(None, 'req'), may hold values from -16 to 16
- query_key_value_weight: bfloat16 [4096, 8, 768], P('req', 'head'), may hold values from -0.1875 to 0.1875
- output_weight: bfloat16 [4096, 4096], P('head', 'req'), may hold values from -0.375 to 0.375
- kv_pool: bfloat16 [4096, 8, 128, 256], P('req', 'head'), may hold values from -68 to 68
- lengths: int32 [512], P('req'), may hold values from 513 to 2048, as said below
- page_table: int32 [512, 16], P('req'), may hold values from 0 to 127, as said below
- send_slots: int32 [4096], P('req'), may hold values from 0 to 63, as said below
Outputs:
- attn_out: bfloat16 [512, 4096], P('head', 'req')
Inputs may be any that keep to these rules, and one draw needn't show every extreme that they name: `page_table`: A request's live positions name distinct slots of its group's store, and every other entry is 0. Slots below 64 are the group's own pool rows; slot 64 + s is the page that group s sends to it. Every group uses exactly 32 of the 64 pages sent to it, never for a long request. `send_slots`: every group sends one page to every group; rows whose page the receiver does not use name an arbitrary slot. In 16 of the groups one request is long (more than (15) * 128 tokens); all others hold at most 768 tokens. The new token sits at position lengths[r].
All inputs are finite; a program needn't handle non-finite values.
Results may differ from a plain program's by a relative error of at most 0.018.
Values may be sent and summed in bfloat16 or wider, within the bound.
A program may use at most 64 MiB of HBM per device.

v0:
```python
import jax
import jax.numpy as jnp
from jax import lax
from jax.sharding import PartitionSpec as P

ROPE_BASE = 500000.0
NEG_FILL = -1e30


def rotate(vectors, angles):
    half_width = vectors.shape[-1] // 2
    first_half = vectors[..., :half_width]
    second_half = vectors[..., half_width:]
    cosine = jnp.cos(angles)
    sine_part = jnp.sin(angles)
    return jnp.concatenate(
        [
            first_half * cosine - second_half * sine_part,
            second_half * cosine + first_half * sine_part,
        ],
        axis=-1,
    )


def rope_angles(lengths, width):
    exponent = jnp.arange(width // 2, dtype=jnp.float32) * (2.0 / width)
    inverse = 1.0 / ROPE_BASE**exponent
    return lengths.astype(jnp.float32)[:, None] * inverse[None, :]


def split_projection(projected_rows, lengths):
    angles = rope_angles(lengths, projected_rows.shape[-1])
    queries = rotate(projected_rows[:, :, :-2], angles[:, None, None, :]).astype(jnp.bfloat16)
    new_keys = rotate(projected_rows[:, :, -2], angles[:, None, :]).astype(jnp.bfloat16)
    new_values = projected_rows[:, :, -1].astype(jnp.bfloat16)
    return (queries, new_keys, new_values)


def page_stats(queries, pages, valid_tokens, score_scale):
    head_dim = pages.shape[-1] // 2
    scores = (
        jnp.einsum(
            "nhqd,nhtd->nhqt", queries, pages[..., :head_dim], preferred_element_type=jnp.float32
        )
        * score_scale
    )
    token_mask = jnp.arange(pages.shape[2])[None, None, None, :] < valid_tokens[:, None, None, None]
    masked = jnp.where(token_mask, scores, NEG_FILL)
    top_score = jnp.max(masked, axis=-1)
    weights = jnp.where(token_mask, jnp.exp(scores - top_score[..., None]), 0.0)
    weight_sum = jnp.sum(weights, axis=-1)
    weighted_values = jnp.einsum(
        "nhqt,nhtd->nhqd",
        weights.astype(jnp.bfloat16),
        pages[..., head_dim:],
        preferred_element_type=jnp.float32,
    )
    return (top_score, weight_sum, weighted_values)


def shards(hidden, query_key_value_weight, output_weight, kv_pool, lengths, page_table, send_slots):
    groups = lax.axis_size("req")
    local_count = lengths.shape[0]
    head_count = query_key_value_weight.shape[1]
    pool_slots = kv_pool.shape[0]
    page_len = kv_pool.shape[2]
    head_dim = kv_pool.shape[3] // 2
    per_head = query_key_value_weight.shape[2] // head_dim
    flat_weight = query_key_value_weight.reshape(
        query_key_value_weight.shape[0], head_count * per_head * head_dim
    )
    projected_rows = lax.psum_scatter(
        jnp.dot(hidden, flat_weight, preferred_element_type=jnp.float32),
        "req",
        scatter_dimension=0,
        tiled=True,
    )
    projected_rows = projected_rows.reshape(local_count, head_count, per_head, head_dim)
    queries, new_keys, new_values = split_projection(projected_rows, lengths)
    score_scale = head_dim ** (-0.5)
    self_scores = (
        jnp.sum(queries.astype(jnp.float32) * new_keys.astype(jnp.float32)[:, :, None, :], axis=-1)
        * score_scale
    )
    total_slots = pool_slots + groups
    places = jnp.arange(page_table.shape[1], dtype=jnp.int32)
    is_live = places[None, :] * page_len < lengths[:, None]
    tokens_in = jnp.clip(lengths[:, None] - places[None, :] * page_len, 0, page_len)
    table_hits = (
        page_table[:, :, None] == jnp.arange(total_slots, dtype=jnp.int32)[None, None, :]
    ) & is_live[:, :, None]
    owner_map = jnp.any(table_hits, axis=1).T
    valid_tokens = jnp.sum(jnp.where(table_hits, tokens_in[:, :, None], 0), axis=(0, 1))
    owner_index = jnp.sum(
        jnp.where(owner_map, jnp.arange(local_count, dtype=jnp.int32)[None, :], 0), axis=1
    )
    slot_queries = jnp.einsum(
        "nr,rhqd->nhqd", owner_map.astype(jnp.bfloat16), queries, preferred_element_type=jnp.float32
    ).astype(jnp.bfloat16)
    outgoing = kv_pool[send_slots]
    arrived = lax.all_to_all(outgoing, "req", split_axis=0, concat_axis=0, tiled=True)
    page_store = jnp.concatenate([kv_pool, arrived], axis=0)
    page_max, page_sum, page_acc = page_stats(slot_queries, page_store, valid_tokens, score_scale)
    owned_max = jnp.max(jnp.where(owner_map[:, :, None, None], page_max[:, None], NEG_FILL), axis=0)
    top_score = jnp.maximum(owned_max, self_scores)
    factors = jnp.exp(page_max - top_score[owner_index])
    owner_float = owner_map.astype(jnp.float32)
    self_weight = jnp.exp(self_scores - top_score)
    total_weight_sum = (
        jnp.einsum("nr,nhq->rhq", owner_float, factors * page_sum, precision=lax.Precision.HIGHEST)
        + self_weight
    )
    weighted_values = jnp.einsum(
        "nr,nhqd->rhqd", owner_float, factors[..., None] * page_acc, precision=lax.Precision.HIGHEST
    )
    weighted_values = (
        weighted_values + self_weight[..., None] * new_values.astype(jnp.float32)[:, :, None, :]
    )
    output_per_head = (
        (weighted_values / total_weight_sum[..., None])
        .astype(jnp.bfloat16)
        .reshape(local_count, head_count * (per_head - 2) * head_dim)
    )
    partial_out = jnp.dot(
        lax.all_gather(output_per_head, "req", axis=0, tiled=True),
        output_weight,
        preferred_element_type=jnp.float32,
    )
    return lax.psum_scatter(
        partial_out.astype(jnp.bfloat16), "head", scatter_dimension=0, tiled=True
    )


def solution(mesh):
    return jax.shard_map(
        shards,
        mesh=mesh,
        in_specs=(
            P(None, "req"),
            P("req", "head", None),
            P("head", "req"),
            P("req", "head", None, None),
            P("req"),
            P("req", None),
            P("req"),
        ),
        out_specs=P("head", "req"),
        check_vma=False,
    )
```

profile of v0, /device:TPU:2, one launch (start us, length us, event | category | flops | bytes accessed | tf_op | source)
XLA Modules:
  0.0 291.1 jit_solution(14235447509010207527)
XLA Ops:
  6.5 0.0 copy-start
  6.5 0.7 compare_select_fusion.1
  7.2 5.0 %gather_fusion = bf16[64,128,256]{2,1,0:T(8,128)(2,1)} fusion(bf16[64,128,256]{2,1,0:T(8,128)(2,1)} %bitcast.50, s32[1024]{0:T(1024)S(1)} %pad_clamp_fusion.1), kind=kCustom, calls=%fused_computation | custom fusion | bytes 8388864 | tf_op jit(solution)/shard_map/gather | solution.py:100
  12.2 0.0 copy-start.2
  12.2 0.0 copy-start.4
  12.2 0.0 copy-start.3
  12.2 11.1 %all-to-all-start = ((bf16[64,1,128,256]{3,2,1,0:T(8,128)(2,1)}), bf16[64,1,128,256]{3,2,1,0:T(8,128)(2,1)}, u32[]{:S(2)}, u32[]{:S(2)}) async-start(bf16[64,1,128,256]{3,2,1,0:T(8,128)(2,1)} %bitcast.53), calls=%async_computation.1 | async-start | bytes 8388608 | tf_op jit(solution)/shard_map/all_to_all | solution.py:101
  23.4 0.0 reduce-scatter.3.cloned.1.call-start
  23.4 0.0 copy-done
  23.4 0.0 copy-done.2
  23.4 1.6 fusion.25
  25.0 0.0 reduce-scatter.3.cloned.1.call-update
  25.1 0.0 reduce-scatter.5.cloned.1.call-start
  25.1 0.0 copy-done.4
  25.2 0.1 broadcast_compare_fusion
  25.2 0.0 copy-done.3
  25.2 0.1 fusion.29
  25.4 0.1 subtract_clamp_fusion
  25.5 0.1 select_reduce_fusion.1
  25.6 0.1 multiply_cosine_fusion.1
  25.7 0.1 iota_compare_fusion
  25.8 155.3 %reduce-scatter.3.cloned.1.call-done = f32[8,768]{1,0:T(8,128)} async-done(((f32[512,768]{1,0:T(8,128)}), f32[8,768]{1,0:T(8,128)}) %reduce-scatter.3.cloned.1.call-update) | async-done | bytes 24592 | tf_op jit(solution)/shard_map/reduce_scatter | solution.py:72
  181.1 0.7 slice_bitcast_fusion
  181.8 0.1 fusion.46
  181.9 0.1 maximum_convert_fusion
  182.0 0.9 subtract_convert_fusion
  182.9 0.2 multiply_reduce_fusion
  183.0 0.7 fusion.44
  183.7 0.3 convolution_convert_fusion.1
  184.0 0.0 all-to-all-done
  184.0 4.6 %select_reduce_fusion = (f32[128,4]{1,0:T(8,128)S(1)}, f32[128,4,128]{2,1,0:T(4,128)S(1)}) fusion(pred[128,128]{1,0:T(8,128)(4,1)S(1)} %iota_compare_fusion, bf16[64,1,128,256]{3,2,0,1:T(8,128)(2,1)} %bitcast.51, bf16[64,1,128,256]{3,2,0,1:T(8,128)(2,1)} %bitcast.8, bf16[128,4,128]{2,0,1:T(8,128)(2,1)S(1)} %convolution_convert_fusion.1), kind=kOutput, calls=%fused_computation.22 | convolution fusion | flops 19070464 | bytes 8800256 | tf_op jit(solution)/shard_map/nhqd,nhtd->nhqt/dot_general | solution.py:42
  188.6 0.1 copy.20
  188.6 0.1 select_reduce_fusion.2
  188.8 0.1 copy.21
  188.8 0.7 gather_fusion.1
  189.5 0.4 fusion.18
  189.9 0.0 copy-start.1
  189.9 3.5 %fusion.11 = f32[128,4,128]{2,1,0:T(4,128)S(1)} fusion(bf16[64,1,128,256]{3,2,0,1:T(8,128)(2,1)} %bitcast.8, bf16[64,1,128,256]{3,2,0,1:T(8,128)(2,1)} %bitcast.52, f32[128,4,128]{2,1,0:T(4,128)S(1)} %get-tuple-element.14, f32[128,4]{1,0:T(8,128)S(1)} %get-tuple-element.13, f32[128,4]{1,0:T(8,128)S(1)} %subtract_exponential_fusion, ...), kind=kOutput, calls=%fused_computation.12 | convolution fusion | flops 25427968 | bytes 8933376 | tf_op jit(solution)/shard_map/nhqt,nhtd->nhqd/dot_general | solution.py:52
  193.4 0.2 convolution_add_fusion.1
  193.6 0.2 fusion.16
  193.9 48.6 %all_gather.3 = bf16[512,512]{1,0:T(8,128)(2,1)S(1)} all-gather(bf16[8,512]{1,0:T(8,128)(2,1)S(1)} %fusion.16), channel_id=1, replica_groups=mesh['req'=64,'head'=8] {'req'}, dimensions={0}, use_global_device_ids=true | all-gather | bytes 532480 | tf_op jit(solution)/shard_map/all_gather | solution.py:125
  242.5 0.0 copy-done.1
  242.5 0.9 convolution_convert_fusion
  243.4 0.0 reduce-scatter.5.cloned.1.call-update
  243.4 40.8 %reduce-scatter.5.cloned.1.call-done = bf16[64,64]{1,0:T(8,128)(2,1)} async-done(((bf16[512,64]{1,0:T(8,128)(2,1)}), bf16[64,64]{1,0:T(8,128)(2,1)}) %reduce-scatter.5.cloned.1.call-update) | async-done | bytes 8208 | tf_op jit(solution)/shard_map/reduce_scatter | solution.py:129
  (9 shorter events, 0.1 us)
Async XLA Ops:
  6.5 16.9 %copy-start = (bf16[64,1,768]{2,0,1:T(8,128)(2,1)S(1)}, bf16[64,1,768]{2,0,1:T(8,128)(2,1)}, u32[]{:S(2)}) copy-start(bf16[64,1,768]{2,0,1:T(8,128)(2,1)} %param.8) | copy-start | bytes 294916
  12.2 11.2 %copy-start.2 = (bf16[512,64]{0,1:T(8,128)(2,1)S(1)}, bf16[512,64]{0,1:T(8,128)(2,1)}, u32[]{:S(2)}) copy-start(bf16[512,64]{0,1:T(8,128)(2,1)} %param.7) | copy-start | bytes 196612
  12.2 12.9 %copy-start.4 = (s32[8]{0:T(128)S(1)}, s32[8]{0:T(128)}, u32[]{:S(2)}) copy-start(s32[8]{0:T(128)} %param.11) | copy-start | bytes 100
  12.2 13.0 %copy-start.3 = (s32[8,16]{1,0:T(8,128)S(1)}, s32[8,16]{1,0:T(8,128)}, u32[]{:S(2)}) copy-start(s32[8,16]{1,0:T(8,128)} %param.12) | copy-start | bytes 1540
  12.2 171.8 %all-to-all-start = ((bf16[64,1,128,256]{3,2,1,0:T(8,128)(2,1)}), bf16[64,1,128,256]{3,2,1,0:T(8,128)(2,1)}, u32[]{:S(2)}, u32[]{:S(2)}) async-start(bf16[64,1,128,256]{3,2,1,0:T(8,128)(2,1)} %bitcast.53), calls=%async_computation.1 | async-start | bytes 8388608 | tf_op jit(solution)/shard_map/all_to_all | solution.py:101
  23.4 157.7 %reduce-scatter.3.cloned.1.call-start = ((), (), s32[]{:S(2)}) async-start(), calls=%async_computation.3 | async-start | bytes 1597440 | tf_op jit(solution)/shard_map/reduce_scatter | solution.py:72
  25.1 259.2 %reduce-scatter.5.cloned.1.call-start = ((), (), s32[]{:S(2)}) async-start(), calls=%async_computation.4 | async-start | bytes 147456 | tf_op jit(solution)/shard_map/reduce_scatter | solution.py:129
  189.9 52.6 %copy-start.1 = (bf16[512,64]{0,1:T(8,128)(2,1)S(1)}, bf16[512,64]{0,1:T(8,128)(2,1)}, u32[]{:S(2)}) copy-start(bf16[512,64]{0,1:T(8,128)(2,1)} %param.9) | copy-start | bytes 196612
Sparse Core Ops, SparseCore 0:
  28.8 152.2 reduce-scatter.2
  243.6 40.6 reduce-scatter.4
where the time goes:
time: 292 us; the launch traced here: 291 us
  waiting for transfers between devices  196 us (67%)
  blocking collectives  48.6 us (17%)
  between operations  13.5 us (5%)
  matrix products  11.3 us (4%)
  starting transfers between devices  11.2 us (4%)
  local copies, waits for them, and re-layouts  6.47 us (2%)
  other arithmetic  3.76 us (1%)
    reduce_scatter x1, waiting for transfers between devices, shards(): lax.psum_scatter(jnp.dot(hidden, flat_weight, preferred_element_type=jnp....  155 us
    all_gather x1, blocking collectives, shards(): lax.all_gather(output_per_head, 'req', axis=0, tiled=True)  48.6 us
    reduce_scatter x1, waiting for transfers between devices, shards(): lax.psum_scatter(partial_out.astype(jnp.bfloat16), 'head', scatter_dimens...  40.8 us
    all_to_all x1, starting transfers between devices, shards(): lax.all_to_all(outgoing, 'req', split_axis=0, concat_axis=0, tiled=True)  11.1 us
  transfers between devices with their start and end apart: 3, of which 2 were waited for; matrix products, arithmetic and copies ran while one was open for 2% of the time, Pallas kernels for 0%

commit v1 on v0

--- a/solution.py
+++ b/solution.py
@@ -1,3 +1,4 @@
+import functools
 import jax
 import jax.numpy as jnp
 from jax import lax
@@ -5,6 +6,17 @@
 
 ROPE_BASE = 500000.0
 NEG_FILL = -1e30
+
+
+def _make_trails(incoming_x, k_dim):
+    n_parts = lax.axis_size("req")
+    blocks_here = [n_parts if kk == k_dim else 1 for kk in range(incoming_x.ndim)]
+    return lax.all_to_all(
+        jnp.tile(incoming_x, blocks_here), "req", split_axis=k_dim, tiled=True, concat_axis=k_dim
+    )
+
+
+_lay_sides = functools.partial(_make_trails, k_dim=0)
 
 
 def rotate(vectors, angles):
@@ -122,9 +134,7 @@
         .reshape(local_count, head_count * (per_head - 2) * head_dim)
     )
     partial_out = jnp.dot(
-        lax.all_gather(output_per_head, "req", axis=0, tiled=True),
-        output_weight,
-        preferred_element_type=jnp.float32,
+        _lay_sides(output_per_head), output_weight, preferred_element_type=jnp.float32
     )
     return lax.psum_scatter(
         partial_out.astype(jnp.bfloat16), "head", scatter_dimension=0, tiled=True

time: 292 us -> 266 us (0.911)
  blocking collectives: 48.6 us -> 25.1 us
    all_gather x1 -> x0, blocking collectives: 48.6 us -> none  [shards(): lax.all_gather(output_per_head, 'req', axis=0, tiled=True)]
    all_to_all x0 -> x1, blocking collectives: none -> 25.1 us  [_make_trails(): lax.all_to_all(jnp.tile(incoming_x, blocks_here), 'req', split_axis=k_dim...]
where the time goes in v1:
time: 266 us; the launch traced here: 265 us
  waiting for transfers between devices  194 us (73%)
  blocking collectives  25.1 us (9%)
  between operations  13.5 us (5%)
  matrix products  11.3 us (4%)
  starting transfers between devices  11.2 us (4%)
  local copies, waits for them, and re-layouts  6.51 us (2%)
  other arithmetic  3.76 us (1%)
    reduce_scatter x1, waiting for transfers between devices, shards(): lax.psum_scatter(jnp.dot(hidden, flat_weight, preferred_element_type=jnp....  155 us
    reduce_scatter x1, waiting for transfers between devices, shards(): lax.psum_scatter(partial_out.astype(jnp.bfloat16), 'head', scatter_dimens...  38.5 us
    all_to_all x1, blocking collectives, _make_trails(): lax.all_to_all(jnp.tile(incoming_x, blocks_here), 'req', split_axis=k_dim...  25.1 us
    all_to_all x1, starting transfers between devices, shards(): lax.all_to_all(outgoing, 'req', split_axis=0, concat_axis=0, tiled=True)  11.1 us
  transfers between devices with their start and end apart: 3, of which 2 were waited for; matrix products, arithmetic and copies ran while one was open for 2% of the time, Pallas kernels for 0%

profile of v1, /device:TPU:2, one launch (start us, length us, event | category | flops | bytes accessed | tf_op | source)
XLA Modules:
  0.0 265.3 jit_solution(14369854928838752136)
XLA Ops:
  6.5 0.0 copy-start
  6.5 0.7 compare_select_fusion.1
  7.2 5.0 %gather_fusion = bf16[64,128,256]{2,1,0:T(8,128)(2,1)} fusion(bf16[64,128,256]{2,1,0:T(8,128)(2,1)} %bitcast.52, s32[1024]{0:T(1024)S(1)} %pad_clamp_fusion.1), kind=kCustom, calls=%fused_computation | custom fusion | bytes 8388864 | tf_op jit(solution)/shard_map/gather | solution.py:112
  12.2 0.0 copy-start.2
  12.2 0.0 copy-start.4
  12.2 0.0 copy-start.3
  12.2 11.1 %all-to-all-start = ((bf16[64,1,128,256]{3,2,1,0:T(8,128)(2,1)}), bf16[64,1,128,256]{3,2,1,0:T(8,128)(2,1)}, u32[]{:S(2)}, u32[]{:S(2)}) async-start(bf16[64,1,128,256]{3,2,1,0:T(8,128)(2,1)} %bitcast.55), calls=%async_computation.1 | async-start | bytes 8388608 | tf_op jit(solution)/shard_map/all_to_all | solution.py:113
  23.4 0.0 reduce-scatter.3.cloned.1.call-start
  23.4 0.0 copy-done
  23.4 0.0 copy-done.2
  23.4 1.6 fusion.26
  25.0 0.0 reduce-scatter.3.cloned.1.call-update
  25.1 0.0 reduce-scatter.5.cloned.1.call-start
  25.1 0.0 copy-done.4
  25.2 0.1 broadcast_compare_fusion
  25.2 0.0 copy-done.3
  25.2 0.1 fusion.30
  25.4 0.1 subtract_clamp_fusion
  25.5 0.1 select_reduce_fusion.1
  25.6 0.1 multiply_cosine_fusion.1
  25.7 0.1 iota_compare_fusion
  25.8 155.3 %reduce-scatter.3.cloned.1.call-done = f32[8,768]{1,0:T(8,128)} async-done(((f32[512,768]{1,0:T(8,128)}), f32[8,768]{1,0:T(8,128)}) %reduce-scatter.3.cloned.1.call-update) | async-done | bytes 24592 | tf_op jit(solution)/shard_map/reduce_scatter | solution.py:84
  181.1 0.7 slice_bitcast_fusion
  181.8 0.1 fusion.47
  181.9 0.1 maximum_convert_fusion
  182.0 0.9 subtract_convert_fusion
  182.9 0.2 multiply_reduce_fusion
  183.0 0.7 fusion.45
  183.7 0.3 convolution_convert_fusion.1
  184.0 0.0 all-to-all-done
  184.0 4.6 %select_reduce_fusion = (f32[128,4]{1,0:T(8,128)S(1)}, f32[128,4,128]{2,1,0:T(4,128)S(1)}) fusion(pred[128,128]{1,0:T(8,128)(4,1)S(1)} %iota_compare_fusion, bf16[64,1,128,256]{3,2,0,1:T(8,128)(2,1)} %bitcast.53, bf16[64,1,128,256]{3,2,0,1:T(8,128)(2,1)} %bitcast.8, bf16[128,4,128]{2,0,1:T(8,128)(2,1)S(1)} %convolution_convert_fusion.1), kind=kOutput, calls=%fused_computation.23 | convolution fusion | flops 19070464 | bytes 8800256 | tf_op jit(solution)/shard_map/nhqd,nhtd->nhqt/dot_general | solution.py:54
  188.6 0.1 copy.20
  188.6 0.1 select_reduce_fusion.2
  188.8 0.1 copy.21
  188.8 0.7 gather_fusion.1
  189.5 0.4 fusion.19
  189.9 0.0 copy-start.1
  189.9 3.5 %fusion.11 = f32[128,4,128]{2,1,0:T(4,128)S(1)} fusion(bf16[64,1,128,256]{3,2,0,1:T(8,128)(2,1)} %bitcast.8, bf16[64,1,128,256]{3,2,0,1:T(8,128)(2,1)} %bitcast.54, f32[128,4,128]{2,1,0:T(4,128)S(1)} %get-tuple-element.14, f32[128,4]{1,0:T(8,128)S(1)} %get-tuple-element.13, f32[128,4]{1,0:T(8,128)S(1)} %subtract_exponential_fusion, ...), kind=kOutput, calls=%fused_computation.12 | convolution fusion | flops 25427968 | bytes 8933376 | tf_op jit(solution)/shard_map/nhqt,nhtd->nhqd/dot_general | solution.py:64
  193.4 0.2 convolution_add_fusion.1
  193.6 0.2 fusion.16
  193.9 25.1 %all_to_all.14 = bf16[64,8,512]{2,1,0:T(8,128)(2,1)S(1)} all-to-all(bf16[64,8,512]{2,1,0:T(8,128)(2,1)S(1)} %tile.9), channel_id=1, replica_groups=mesh['req'=64,'head'=8] {'req'}, dimensions={0} | all-to-all | bytes 1048576 | tf_op jit(solution)/shard_map/all_to_all | solution.py:14
  219.0 0.0 copy-done.1
  219.0 0.9 convolution_convert_fusion
  219.9 0.0 reduce-scatter.5.cloned.1.call-update
  219.9 38.5 %reduce-scatter.5.cloned.1.call-done = bf16[64,64]{1,0:T(8,128)(2,1)} async-done(((bf16[512,64]{1,0:T(8,128)(2,1)}), bf16[64,64]{1,0:T(8,128)(2,1)}) %reduce-scatter.5.cloned.1.call-update) | async-done | bytes 8208 | tf_op jit(solution)/shard_map/reduce_scatter | solution.py:139
  (10 shorter events, 0.1 us)
Async XLA Ops:
  6.5 16.9 %copy-start = (bf16[64,1,768]{2,0,1:T(8,128)(2,1)S(1)}, bf16[64,1,768]{2,0,1:T(8,128)(2,1)}, u32[]{:S(2)}) copy-start(bf16[64,1,768]{2,0,1:T(8,128)(2,1)} %param.8) | copy-start | bytes 294916
  12.2 11.2 %copy-start.2 = (bf16[512,64]{0,1:T(8,128)(2,1)S(1)}, bf16[512,64]{0,1:T(8,128)(2,1)}, u32[]{:S(2)}) copy-start(bf16[512,64]{0,1:T(8,128)(2,1)} %param.7) | copy-start | bytes 196612
  12.2 12.9 %copy-start.4 = (s32[8]{0:T(128)S(1)}, s32[8]{0:T(128)}, u32[]{:S(2)}) copy-start(s32[8]{0:T(128)} %param.11) | copy-start | bytes 100
  12.2 13.0 %copy-start.3 = (s32[8,16]{1,0:T(8,128)S(1)}, s32[8,16]{1,0:T(8,128)}, u32[]{:S(2)}) copy-start(s32[8,16]{1,0:T(8,128)} %param.12) | copy-start | bytes 1540
  12.2 171.8 %all-to-all-start = ((bf16[64,1,128,256]{3,2,1,0:T(8,128)(2,1)}), bf16[64,1,128,256]{3,2,1,0:T(8,128)(2,1)}, u32[]{:S(2)}, u32[]{:S(2)}) async-start(bf16[64,1,128,256]{3,2,1,0:T(8,128)(2,1)} %bitcast.55), calls=%async_computation.1 | async-start | bytes 8388608 | tf_op jit(solution)/shard_map/all_to_all | solution.py:113
  23.4 157.7 %reduce-scatter.3.cloned.1.call-start = ((), (), s32[]{:S(2)}) async-start(), calls=%async_computation.4 | async-start | bytes 1597440 | tf_op jit(solution)/shard_map/reduce_scatter | solution.py:84
  25.1 233.4 %reduce-scatter.5.cloned.1.call-start = ((), (), s32[]{:S(2)}) async-start(), calls=%async_computation.5 | async-start | bytes 147456 | tf_op jit(solution)/shard_map/reduce_scatter | solution.py:139
  189.9 29.1 %copy-start.1 = (bf16[512,64]{0,1:T(8,128)(2,1)S(1)}, bf16[512,64]{0,1:T(8,128)(2,1)}, u32[]{:S(2)}) copy-start(bf16[512,64]{0,1:T(8,128)(2,1)} %param.9) | copy-start | bytes 196612
Sparse Core Ops, SparseCore 0:
  28.8 152.2 reduce-scatter.2
  220.1 38.3 reduce-scatter.4
